TPU v7x, 32 devices: a whole 2x2x4 slice. The times are simulated.
32 devices in a mesh: brick: 16 (over z, y, x), seed: 2 (over core).
Axes of the slice: x: 2, y: 2, z: 4, core: 2. Of those that a mesh axis runs over, the one named last changes fastest.
Arguments:
- seed_data: float32 [4, 65536], P(None, ('brick', 'seed')), as said below
- block_slot: int32 [512], replicated, may hold values from 0 to 511, as said below
- candidates: int32 [256, 8], P('brick', 'seed'), may hold values from 0 to 511, as said below
- cand_count: int32 [256], P('brick'), may hold values from 1 to 8
- pixel_mass: float32 [256, 512], P('brick'), may hold values from 0.1 to 1
Outputs:
- seed_stats: float32 [4, 65536], P(None, ('brick', 'seed'))
Inputs may be any that keep to these rules, and one draw needn't show every extreme that they name: A permutation of the storage positions. Block g is homed in brick g // 32 and stored on the device of brick index block_slot[g] // 32 and seed index (block_slot[g] // 16) % 2. For each brick and seed index, exactly 16 blocks homed in that brick are stored at that seed index; one device stores at most 1 block homed in any one brick, and some devices reach it. `candidates`: row t holds 8 distinct ids of blocks homed in tile t's brick, between (t // 16) * 32 and that plus 32 - 1. `seed_data`: the seeds of a block lie in the region of its home brick: second coordinate between h * 2 and (h + 1) * 2 for home brick h, first between 0 and 1, third between 0 and 8.
All inputs are finite; a program needn't handle non-finite values.
Results may differ from a plain program's by a relative error of at most 0.0003.
Values sent between devices are 32-bit elements; how exact they have to be, the bound alone decides.
No kernel may reach another device: no remote copies, remote signals or barrier semaphores. Data moves between devices by JAX's collectives and lax.ppermute only.
A program may use at most 64 MiB of HBM per device.

v0:
```python
import math
import jax
import jax.numpy as jnp
from jax import lax
from jax.sharding import PartitionSpec as P

TILES_Y = 2
TILES_Z = 8
blur_eps = 0.5
far_score = -1e30


def joined(value, axis, join):
    pieces = jax.tree.map(lambda part: lax.all_gather(part, axis), value)
    head = jax.tree.map(lambda part: part[0], pieces)
    tail = jax.tree.map(lambda part: part[1:], pieces)
    running, _ = lax.scan(lambda running, share: (join(running, share), None), head, tail)
    return running


def pixel_points(brick_ids, tile_ids):
    within = jnp.arange(512, dtype=jnp.int32)
    tile_x = tile_ids // (TILES_Y * TILES_Z)
    tile_y = tile_ids // TILES_Z % TILES_Y
    tile_z = tile_ids % TILES_Z
    offset_x = ((within // 64).astype(jnp.float32) + 0.5) / 8.0
    offset_y = ((within // 8 % 8).astype(jnp.float32) + 0.5) / 8.0
    offset_z = ((within % 8).astype(jnp.float32) + 0.5) / 8.0
    point_x = tile_x.astype(jnp.float32)[:, None] + offset_x[None, :]
    point_y = (brick_ids * TILES_Y + tile_y).astype(jnp.float32)[:, None] + offset_y[None, :]
    point_z = tile_z.astype(jnp.float32)[:, None] + offset_z[None, :]
    return jnp.stack([point_x, point_y, point_z])


def tile_scores(points, seed_cols, valid_cols):
    differ = points[0][:, :, None] - seed_cols[0][:, None, :]
    distance = differ * differ
    differ = points[1][:, :, None] - seed_cols[1][:, None, :]
    distance = distance + differ * differ
    differ = points[2][:, :, None] - seed_cols[2][:, None, :]
    distance = distance + differ * differ
    scores = (seed_cols[3][:, None, :] - distance) / blur_eps
    return jnp.where(valid_cols[:, None, :], scores, far_score)


def combine_stats(left_pair, right_pair):
    left_peak, left_total = left_pair
    right_peak, right_total = right_pair
    joint_peak = jnp.maximum(left_peak, right_peak)
    joint_total = left_total * jnp.exp(left_peak - joint_peak) + right_total * jnp.exp(
        right_peak - joint_peak
    )
    return (joint_peak, joint_total)


def body(seed_data, block_slot, candidates, cand_count, pixel_mass):
    brick_index = lax.axis_index("brick")
    shard_index = lax.axis_index("seed")
    brick_size = lax.axis_size("brick")
    seed_size = lax.axis_size("seed")
    lane_count = seed_data.shape[1] // 128
    home_blocks = lane_count * seed_size
    total_blocks = block_slot.shape[0]
    capacity = max(1, lane_count // brick_size)
    tile_count, slot_count = candidates.shape
    positions = jnp.arange(total_blocks, dtype=jnp.int32)
    inverse = jnp.zeros((total_blocks,), jnp.int32).at[block_slot].set(positions)
    home_of_pos = inverse // home_blocks
    grouped = home_of_pos.reshape(brick_size * seed_size, lane_count)
    lane_ids = jnp.arange(lane_count, dtype=jnp.int32)
    before = lane_ids[:, None] < lane_ids[None, :]
    same_home = grouped[:, :, None] == grouped[:, None, :]
    rank_of_pos = jnp.sum(same_home & before[None], axis=1).reshape(total_blocks)
    own_first = (brick_index * seed_size + shard_index) * lane_count
    own_home = lax.dynamic_slice_in_dim(home_of_pos, own_first, lane_count)
    own_rank = lax.dynamic_slice_in_dim(rank_of_pos, own_first, lane_count)
    own_seeds = seed_data.reshape(4, lane_count, 128)
    outgoing = jnp.zeros((4, brick_size * capacity, 128), jnp.float32)
    outgoing = outgoing.at[:, own_home * capacity + own_rank, :].set(own_seeds)
    incoming = lax.all_to_all(outgoing, "brick", split_axis=1, concat_axis=1, tiled=True)
    home_slots = lax.dynamic_slice_in_dim(block_slot, brick_index * home_blocks, home_blocks)
    home_shard = home_slots // lane_count % seed_size
    home_owner = home_slots // home_blocks
    home_rank = rank_of_pos[home_slots]
    home_flat = home_owner * capacity + home_rank
    members = jnp.arange(home_blocks, dtype=jnp.int32)
    earlier = members[:, None] < members[None, :]
    queue_pos = jnp.sum((home_shard[:, None] == home_shard[None, :]) & earlier, axis=0)
    panel_index = home_shard * lane_count + queue_pos
    is_mine = home_shard == shard_index
    target = jnp.where(is_mine, queue_pos, lane_count)
    compact = jnp.zeros((4, lane_count, 128), jnp.float32)
    compact = compact.at[:, target, :].set(incoming[:, home_flat, :], mode="drop")
    seed_panel = lax.all_gather(compact, "seed", axis=1, tiled=True)
    start_totals = jnp.zeros((4, home_blocks, 128), jnp.float32)
    group_size = math.gcd(tile_count, 8)
    step_count = tile_count // group_size
    slot_cols = slot_count * 128
    slot_ids = shard_index * slot_count + jnp.arange(slot_count, dtype=jnp.int32)
    cand_panel = panel_index[candidates - brick_index * home_blocks]
    valid_all = jnp.repeat(slot_ids[None, :] < cand_count[:, None], 128, axis=1)
    brick_ids = jnp.zeros((group_size,), jnp.int32) + brick_index

    def group_scores(step_index):
        first_tile = step_index * group_size
        tile_ids = first_tile + jnp.arange(group_size, dtype=jnp.int32)
        points = pixel_points(brick_ids, tile_ids)
        chosen = lax.dynamic_slice_in_dim(cand_panel, first_tile, group_size)
        seed_cols = seed_panel[:, chosen.reshape(-1), :].reshape(4, group_size, slot_cols)
        valid_cols = lax.dynamic_slice_in_dim(valid_all, first_tile, group_size)
        return (tile_scores(points, seed_cols, valid_cols), points, chosen, valid_cols)

    def local_both(step_index):
        scores, points, chosen, valid_cols = group_scores(step_index)
        pixel_peak = jnp.max(scores, axis=2)
        raw_share = jnp.where(valid_cols[:, None, :], jnp.exp(scores - pixel_peak[:, :, None]), 0.0)
        return (pixel_peak, jnp.sum(raw_share, axis=2))

    step_ids = jnp.arange(step_count, dtype=jnp.int32)
    peak_local, total_local = lax.map(local_both, step_ids)
    pixel_peak, pixel_total = joined((peak_local, total_local), "seed", combine_stats)

    def contribute(totals, step_bits):
        step_index, group_peak, group_total = step_bits
        scores, points, chosen, valid_cols = group_scores(step_index)
        raw_share = jnp.where(valid_cols[:, None, :], jnp.exp(scores - group_peak[:, :, None]), 0.0)
        shares = raw_share / group_total[:, :, None]
        pixel_weight = lax.dynamic_slice_in_dim(pixel_mass, step_index * group_size, group_size)
        features = jnp.stack(
            [
                pixel_weight,
                pixel_weight * points[0],
                pixel_weight * points[1],
                pixel_weight * points[2],
            ]
        )
        moments = jnp.einsum("fgi,gic->fgc", features, shares, precision=lax.Precision.HIGHEST)
        totals = totals.at[:, chosen.reshape(-1), :].add(
            moments.reshape(4, group_size * slot_count, 128)
        )
        return (totals, None)

    totals, unused = lax.scan(contribute, start_totals, (step_ids, pixel_peak, pixel_total))
    raw_target = home_owner * (seed_size * capacity) + home_shard * capacity + home_rank
    outgoing_raw = jnp.zeros((4, brick_size * seed_size * capacity, 128), jnp.float32)
    outgoing_raw = outgoing_raw.at[:, raw_target, :].set(totals[:, panel_index, :])
    arrived = lax.all_to_all(outgoing_raw, "brick", split_axis=1, concat_axis=1, tiled=True)
    arrived = arrived.reshape(4, brick_size, seed_size * capacity, 128)
    summed_raw = lax.psum_scatter(arrived, "seed", scatter_dimension=2, tiled=True)
    own_rows = summed_raw[:, own_home, own_rank, :]
    mass_row = own_rows[0]
    moment_rows = own_rows[1:4] - mass_row[None] * own_seeds[0:3]
    result = jnp.concatenate([mass_row[None], moment_rows], axis=0)
    return result.reshape(4, lane_count * 128)


def solution(mesh):
    placed = (P(None, ("brick", "seed")), P(), P("brick", "seed"), P("brick"), P("brick", None))
    return jax.shard_map(
        body, mesh=mesh, in_specs=placed, out_specs=P(None, ("brick", "seed")), check_vma=False
    )
```

profile of v0, /device:TPU:0, one launch (start us, length us, event | category | flops | bytes accessed | tf_op | source)
XLA Modules:
  0.0 127.0 jit_solution(10801698994256494854)
XLA Ops:
  6.5 0.7 compare_select_fusion.7
  7.2 2.4 %scatter_custom_fusion.1 = s32[512]{0:T(512)S(1)} fusion(s32[512]{0:T(512)S(1)} %compare_select_fusion.7, s32[512]{0:T(512)S(1)} %iota.132, s32[]{:T(128)} %constant.488.clone.1), kind=kCustom, calls=%fused_computation.207 | custom fusion | bytes 2052 | tf_op jit(solution)/shard_map/scatter | solution.py:67
  9.8 0.1 convert_reduce_fusion
  10.2 0.6 broadcast.1155.clone
  10.8 2.2 %scatter_fusion.1 = f32[4,16,128]{2,0,1:T(4,128)} fusion(f32[4,16,128]{2,0,1:T(4,128)} %broadcast.1155.clone, s32[16]{0:T(128)S(1)} %get-tuple-element.468, f32[16,4,128]{2,1,0:T(4,128)S(1)} %bitcast.70), kind=kCustom, calls=%fused_computation.9 | custom fusion | bytes 98368 | tf_op jit(solution)/shard_map/scatter | solution.py:79
  13.0 8.3 %all-to-all-start = ((f32[4,16,128]{2,0,1:T(4,128)}), f32[4,16,128]{2,0,1:T(4,128)S(1)}, u32[]{:S(2)}, u32[]{:S(2)}) async-start(f32[4,16,128]{2,0,1:T(4,128)} %scatter_fusion.1), calls=%async_computation | async-start | bytes 65536 | tf_op jit(solution)/shard_map/all_to_all | solution.py:80
  21.5 0.7 gather_fusion.2
  22.3 0.1 compare_select_fusion.14
  22.4 0.1 convert_reduce_fusion.1
  22.6 0.1 reshape.575
  22.7 0.8 gather_fusion.3
  23.8 4.9 %all-to-all-done = f32[4,16,128]{2,0,1:T(4,128)S(1)} async-done(((f32[4,16,128]{2,0,1:T(4,128)}), f32[4,16,128]{2,0,1:T(4,128)S(1)}, u32[]{:S(2)}, u32[]{:S(2)}) %all-to-all-start) | async-done | bytes 32800 | tf_op jit(solution)/shard_map/all_to_all | solution.py:80
  28.7 0.6 gather_fusion.4
  29.3 1.5 %scatter_fusion.2 = f32[4,16,128]{2,0,1:T(4,128)S(1)} fusion(f32[4,16,128]{2,0,1:T(4,128)S(1)} %broadcast.1155, s32[32]{0:T(128)S(1)} %get-tuple-element.469, f32[32,4,128]{2,1,0:T(4,128)S(1)} %gather_fusion.4), kind=kCustom, calls=%fused_computation.10 | custom fusion | bytes 196736 | tf_op jit(solution)/shard_map/scatter | solution.py:93
  30.9 1.9 %all_gather.15 = f32[4,32,128]{2,0,1:T(4,128)S(1)} all-gather(f32[4,16,128]{2,0,1:T(4,128)S(1)} %scatter_fusion.2), channel_id=1, replica_groups=mesh['brick'=16,'seed'=2] {'seed'}, dimensions={1}, use_global_device_ids=true | all-gather | bytes 98304 | tf_op jit(solution)/shard_map/all_gather | solution.py:94
  32.7 34.8 %while.35 = (s32[]{:T(128)}, f32[2,8,512]{2,1,0:T(8,128)S(1)}, f32[2,8,512]{2,1,0:T(8,128)S(1)}, s32[2]{0:T(128)S(1)}, pred[16,512]{1,0:T(8,128)(4,1)S(1)}, /*in...) while((s32[]{:T(128)}, f32[2,8,512]{2,1,0:T(8,128)S(1)}, ...), condition=%wide.region_8.9_spmd.clone, body=%wide.region_5.8_spmd.clone.sunk | while | flops 54553152 | bytes 820639 | solution.py:120
  32.7 0.6 dynamic_slice.117
  34.1 0.6 gather_fusion
  34.7 0.2 slice_reduce_fusion.10
  35.2 4.3 %fusion.113 = f32[8,512]{1,0:T(8,128)S(1)} fusion(f32[8,512]{1,0:T(8,128)S(1)} %sub.605, f32[8,512]{1,0:T(8,128)S(1)} %broadcast_add_fusion.9, f32[8,512]{1,0:T(8,128)S(1)} %sub.606, f32[8,512]{1,0:T(8,128)S(1)} %broadcast_add_fusion.10, f32[8,512]{1,0:T(8,128)S(1)} %sub.607, f32[8,512]{1,0:T(8,128)S(1)} %broadcast_add_fusion.11, ...), kind=kLoop, calls=%fused_computation.16.clone.1 | loop fusion | flops 25161728 | bytes 135168 | tf_op jit(solution)/shard_map/while/body/eval_jaxpr/reduce_max | solution.py:115
  39.6 10.5 %select_reduce_fusion.2 = f32[8,512]{1,0:T(8,128)S(1)} fusion(f32[8,512]{1,0:T(8,128)S(1)} %fusion.113, f32[8,512]{1,0:T(8,128)S(1)} %sub.605, f32[8,512]{1,0:T(8,128)S(1)} %broadcast_add_fusion.9, f32[8,512]{1,0:T(8,128)S(1)} %sub.606, f32[8,512]{1,0:T(8,128)S(1)} %broadcast_add_fusion.10, f32[8,512]{1,0:T(8,128)S(1)} %sub.607, ...), kind=kLoop, calls=%fused_computation.14.clone.1 | loop fusion | flops 29356032 | bytes 151552 | tf_op jit(solution)/shard_map/while/body/eval_jaxpr/reduce_sum | solution.py:117
  50.1 0.6 dynamic_slice.117
  51.5 0.6 gather_fusion
  52.1 0.2 slice_reduce_fusion.10
  52.6 4.3 %fusion.113 = f32[8,512]{1,0:T(8,128)S(1)} fusion(f32[8,512]{1,0:T(8,128)S(1)} %sub.605, f32[8,512]{1,0:T(8,128)S(1)} %broadcast_add_fusion.9, f32[8,512]{1,0:T(8,128)S(1)} %sub.606, f32[8,512]{1,0:T(8,128)S(1)} %broadcast_add_fusion.10, f32[8,512]{1,0:T(8,128)S(1)} %sub.607, f32[8,512]{1,0:T(8,128)S(1)} %broadcast_add_fusion.11, ...), kind=kLoop, calls=%fused_computation.16.clone.1 | loop fusion | flops 25161728 | bytes 135168 | tf_op jit(solution)/shard_map/while/body/eval_jaxpr/reduce_max | solution.py:115
  57.0 10.5 %select_reduce_fusion.2 = f32[8,512]{1,0:T(8,128)S(1)} fusion(f32[8,512]{1,0:T(8,128)S(1)} %fusion.113, f32[8,512]{1,0:T(8,128)S(1)} %sub.605, f32[8,512]{1,0:T(8,128)S(1)} %broadcast_add_fusion.9, f32[8,512]{1,0:T(8,128)S(1)} %sub.606, f32[8,512]{1,0:T(8,128)S(1)} %broadcast_add_fusion.10, f32[8,512]{1,0:T(8,128)S(1)} %sub.607, ...), kind=kLoop, calls=%fused_computation.14.clone.1 | loop fusion | flops 29356032 | bytes 151552 | tf_op jit(solution)/shard_map/while/body/eval_jaxpr/reduce_sum | solution.py:117
  67.5 1.9 %all-gather = f32[4,8,512]{2,1,0:T(8,128)S(1)} all-gather(f32[2,8,512]{2,1,0:T(8,128)S(1)} %get-tuple-element.337), channel_id=2, replica_groups=mesh['brick'=16,'seed'=2] {'seed'}, dimensions={0}, use_global_device_ids=true | all-gather | bytes 98304 | tf_op jit(solution)/shard_map/all_gather | solution.py:14
  69.3 1.8 %all-gather.1 = f32[4,8,512]{2,1,0:T(8,128)S(1)} all-gather(f32[2,8,512]{2,1,0:T(8,128)S(1)} %get-tuple-element.338), channel_id=3, replica_groups=mesh['brick'=16,'seed'=2] {'seed'}, dimensions={0}, use_global_device_ids=true | all-gather | bytes 98304 | tf_op jit(solution)/shard_map/all_gather | solution.py:14
  71.2 0.7 copy-done
  72.0 29.0 %while.36 = (s32[]{:T(128)}, f32[4,32,128]{2,0,1:T(4,128)S(1)}, s32[2]{0:T(128)S(1)}, s32[16,4]{1,0:T(8,128)S(1)}, pred[16,512]{1,0:T(8,128)(4,1)S(1)}, /*index=...) while((s32[]{:T(128)}, f32[4,32,128]{2,0,1:T(4,128)S(1)}, ...), condition=%wide.region_11.12_spmd.clone, body=%wide.region_9.11_spmd.clone.sunk | while | flops 130135552 | bytes 1242671 | solution.py:143
  72.0 0.6 dynamic_slice.121
  73.6 0.6 gather_fusion.1
  74.2 0.2 slice_reduce_fusion.11
  74.5 10.3 %fusion.120 = f32[8,512,4]{1,2,0:T(4,128)S(1)} fusion(f32[8,512]{1,0:T(8,128)S(1)} %get-tuple-element.609, f32[8,512]{1,0:T(8,128)S(1)} %get-tuple-element.610, f32[8,512]{1,0:T(8,128)S(1)} %sub.625, f32[8,512]{1,0:T(8,128)S(1)} %get-tuple-element.617, f32[8,512]{1,0:T(8,128)S(1)} %sub.626, f32[8,512]{1,0:T(8,128)S(1)} %get-tuple-element.619, ...), kind=kOutput, calls=%fused_computation.78.clone.1 | convolution fusion | flops 130072576 | bytes 282624 | tf_op jit(solution)/shard_map/while/body/eval_jaxpr/fgi,gic->fgc/dot_general | solution.py:137
  84.8 1.7 %scatter_fusion = f32[4,32,128]{2,0,1:T(4,128)S(1)} fusion(f32[4,32,128]{2,0,1:T(4,128)S(1)} %get-tuple-element.681, s32[32]{0:T(128)S(1)} %fusion.115, f32[32,4,128]{2,1,0:T(4,128)S(1)} %bitcast.65), kind=kCustom, calls=%fused_computation.7.clone.clone.1 | custom fusion | flops 16384 | bytes 196736 | tf_op jit(solution)/shard_map/while/body/eval_jaxpr/scatter-add | solution.py:138
  86.4 0.6 dynamic_slice.121
  88.1 0.6 gather_fusion.1
  88.7 0.2 slice_reduce_fusion.11
  89.0 10.3 %fusion.120 = f32[8,512,4]{1,2,0:T(4,128)S(1)} fusion(f32[8,512]{1,0:T(8,128)S(1)} %get-tuple-element.609, f32[8,512]{1,0:T(8,128)S(1)} %get-tuple-element.610, f32[8,512]{1,0:T(8,128)S(1)} %sub.625, f32[8,512]{1,0:T(8,128)S(1)} %get-tuple-element.617, f32[8,512]{1,0:T(8,128)S(1)} %sub.626, f32[8,512]{1,0:T(8,128)S(1)} %get-tuple-element.619, ...), kind=kOutput, calls=%fused_computation.78.clone.1 | convolution fusion | flops 130072576 | bytes 282624 | tf_op jit(solution)/shard_map/while/body/eval_jaxpr/fgi,gic->fgc/dot_general | solution.py:137
  99.3 1.7 %scatter_fusion = f32[4,32,128]{2,0,1:T(4,128)S(1)} fusion(f32[4,32,128]{2,0,1:T(4,128)S(1)} %get-tuple-element.681, s32[32]{0:T(128)S(1)} %fusion.115, f32[32,4,128]{2,1,0:T(4,128)S(1)} %bitcast.65), kind=kCustom, calls=%fused_computation.7.clone.clone.1 | custom fusion | flops 16384 | bytes 196736 | tf_op jit(solution)/shard_map/while/body/eval_jaxpr/scatter-add | solution.py:138
  100.9 0.6 gather_fusion.5
  101.6 1.5 %scatter_fusion.3 = f32[4,32,128]{2,0,1:T(4,128)S(1)} fusion(f32[4,32,128]{2,0,1:T(4,128)S(1)} %broadcast.1150, s32[32]{0:T(128)S(1)} %get-tuple-element.452, f32[32,4,128]{2,1,0:T(4,128)S(1)} %gather_fusion.5), kind=kCustom, calls=%fused_computation.11 | custom fusion | bytes 196736 | tf_op jit(solution)/shard_map/scatter | solution.py:146
  103.1 10.1 %all_to_all.10 = f32[4,32,128]{2,0,1:T(4,128)S(1)} all-to-all(f32[4,32,128]{2,0,1:T(4,128)S(1)} %scatter_fusion.3), channel_id=1, replica_groups=mesh['brick'=16,'seed'=2] {'brick'}, dimensions={1} | all-to-all | bytes 131072 | tf_op jit(solution)/shard_map/all_to_all | solution.py:147
  113.2 0.6 copy.38
  113.8 4.3 %reduce-scatter.2.cloned.1.call-done = f32[4,16,1,128]{3,1,0,2:T(8,128)} async-done(((f32[4,16,2,128]{3,1,0,2:T(8,128)}), f32[4,16,1,128]{3,1,0,2:T(8,128)}) %reduce-scatter.2.cloned.1.call-update) | async-done | bytes 32784 | tf_op jit(solution)/shard_map/reduce_scatter | solution.py:149
  118.1 0.8 copy.39
  118.9 0.6 gather_fusion.6
  119.5 0.6 maximum_bitcast_fusion
  (121 shorter events, 2.8 us)
Async XLA Ops:
  9.8 1.0 copy-start.1
  10.8 10.6 %copy-start.2 = (s32[512]{0:T(512)S(1)}, s32[512]{0:T(512)}, u32[]{:S(2)}) copy-start(s32[512]{0:T(512)} %param.10) | copy-start | bytes 6148
  13.0 15.7 %all-to-all-start = ((f32[4,16,128]{2,0,1:T(4,128)}), f32[4,16,128]{2,0,1:T(4,128)S(1)}, u32[]{:S(2)}, u32[]{:S(2)}) async-start(f32[4,16,128]{2,0,1:T(4,128)} %scatter_fusion.1), calls=%async_computation | async-start | bytes 65536 | tf_op jit(solution)/shard_map/all_to_all | solution.py:80
  21.3 96.8 %reduce-scatter.2.cloned.1.call-start = ((), (), s32[]{:S(2)}) async-start(), calls=%async_computation.3 | async-start | bytes 98304 | tf_op jit(solution)/shard_map/reduce_scatter | solution.py:149
  21.5 1.0 copy-start.3
  22.7 0.9 copy-start.4
  71.2 0.8 copy-start
Sparse Core Ops, SparseCore 0:
  114.0 4.1 reduce-scatter.1
where the time goes:
time: 127 us
  other arithmetic  36 us (28%)
  local copies, waits for them, and re-layouts  20.5 us (16%)
  matrix products  20.5 us (16%)
  blocking collectives  15.7 us (12%)
  between operations  13.6 us (11%)
  waiting for transfers between devices  9.24 us (7%)
  starting transfers between devices  8.35 us (7%)
  loops' own time  3.11 us (2%)
    reduce_sum x2, other arithmetic, local_both(): return (pixel_peak, jnp.sum(raw_share, axis=2))  21 us
    dot_general x2, matrix products, contribute(): jnp.einsum('fgi,gic->fgc', features, shares, precision=lax.Precision.HIGH...  20.5 us
    all_to_all x1, blocking collectives, body(): lax.all_to_all(outgoing_raw, 'brick', split_axis=1, concat_axis=1, tiled=...  10.1 us
    reduce_max x2, other arithmetic, local_both(): pixel_peak = jnp.max(scores, axis=2)  8.68 us
    all_to_all x1, starting transfers between devices, body(): lax.all_to_all(outgoing, 'brick', split_axis=1, concat_axis=1, tiled=True)  8.31 us
    all_to_all x1, waiting for transfers between devices, body(): lax.all_to_all(outgoing, 'brick', split_axis=1, concat_axis=1, tiled=True)  4.92 us
    reduce_scatter x1, waiting for transfers between devices, body(): lax.psum_scatter(arrived, 'seed', scatter_dimension=2, tiled=True)  4.3 us
    all_gather x2, blocking collectives, joined(): pieces = jax.tree.map(lambda part: lax.all_gather(part, axis), value)  3.69 us
  transfers between devices with their start and end apart: 2, of which 2 were waited for; matrix products, arithmetic and copies ran while one was open for 2% of the time, Pallas kernels for 0%

commit v1 on v0

--- a/solution.py
+++ b/solution.py
@@ -144,7 +144,26 @@
     raw_target = home_owner * (seed_size * capacity) + home_shard * capacity + home_rank
     outgoing_raw = jnp.zeros((4, brick_size * seed_size * capacity, 128), jnp.float32)
     outgoing_raw = outgoing_raw.at[:, raw_target, :].set(totals[:, panel_index, :])
-    arrived = lax.all_to_all(outgoing_raw, "brick", split_axis=1, concat_axis=1, tiled=True)
+
+    def face_reach(local_array, d_out, where_dim):
+        value_now = lax.axis_size("brick")
+        b_next = lax.axis_index("brick")
+        lower, answer = (value_now, b_next)
+        b_now = local_array.shape[d_out] // lower
+        oldest = jnp.roll(local_array, -answer * b_now, d_out)
+        newest = lax.slice_in_dim(oldest, 0, b_now, axis=d_out)
+        in_order = [newest]
+        for dev_j in range(1, lower):
+            shaped = lax.slice_in_dim(oldest, dev_j * b_now, (dev_j + 1) * b_now, axis=d_out)
+            e_next = lax.ppermute(
+                shaped, axis_name="brick", perm=[(q, (q + dev_j) % lower) for q in range(lower)]
+            )
+            in_order.append(e_next)
+        passed = jnp.concatenate(in_order[::-1], axis=where_dim)
+        out_arr = jnp.roll(passed, (answer + 1) * in_order[0].shape[where_dim], axis=where_dim)
+        return out_arr
+
+    arrived = face_reach(outgoing_raw, 1, 1)
     arrived = arrived.reshape(4, brick_size, seed_size * capacity, 128)
     summed_raw = lax.psum_scatter(arrived, "seed", scatter_dimension=2, tiled=True)
     own_rows = summed_raw[:, own_home, own_rank, :]

time: 127 us -> 148 us (1.17)
  starting transfers between devices: 8.35 us -> 31.8 us
  blocking collectives: 15.7 us -> 5.55 us
  waiting for transfers between devices: 9.24 us -> 16 us
    ppermute x0 -> x15, starting transfers between devices: none -> 23.3 us  [face_reach(): lax.ppermute(shaped, axis_name='brick', perm=[(q, (q + dev_j) % lower) fo...]
    all_to_all x1 -> x0, blocking collectives: 10.1 us -> none  [body(): lax.all_to_all(outgoing_raw, 'brick', split_axis=1, concat_axis=1, tiled=...]
    ppermute x0 -> x15, waiting for transfers between devices: none -> 7.16 us  [face_reach(): lax.ppermute(shaped, axis_name='brick', perm=[(q, (q + dev_j) % lower) fo...]
  transfers between devices with their start and end apart: 2 -> 17, of which waited for: 2 -> 5; matrix products, arithmetic and copies ran while one was open for 2% -> 2% of each run, Pallas kernels for 0% -> 0%
where the time goes in v1:
time: 148 us
  other arithmetic  36.2 us (24%)
  starting transfers between devices  31.8 us (21%)
  local copies, waits for them, and re-layouts  20.6 us (14%)
  matrix products  20.5 us (14%)
  waiting for transfers between devices  16 us (11%)
  between operations  13.7 us (9%)
  blocking collectives  5.55 us (4%)
  loops' own time  3.11 us (2%)
    ppermute x15, starting transfers between devices, face_reach(): lax.ppermute(shaped, axis_name='brick', perm=[(q, (q + dev_j) % lower) fo...  23.3 us
    reduce_sum x2, other arithmetic, local_both(): return (pixel_peak, jnp.sum(raw_share, axis=2))  21 us
    dot_general x2, matrix products, contribute(): jnp.einsum('fgi,gic->fgc', features, shares, precision=lax.Precision.HIGH...  20.5 us
    reduce_max x2, other arithmetic, local_both(): pixel_peak = jnp.max(scores, axis=2)  8.68 us
    all_to_all x1, starting transfers between devices, body(): lax.all_to_all(outgoing, 'brick', split_axis=1, concat_axis=1, tiled=True)  8.44 us
    ppermute x15, waiting for transfers between devices, face_reach(): lax.ppermute(shaped, axis_name='brick', perm=[(q, (q + dev_j) % lower) fo...  7.16 us
    all_to_all x1, waiting for transfers between devices, body(): lax.all_to_all(outgoing, 'brick', split_axis=1, concat_axis=1, tiled=True)  4.89 us
    reduce_scatter x1, waiting for transfers between devices, body(): lax.psum_scatter(arrived, 'seed', scatter_dimension=2, tiled=True)  3.91 us
  transfers between devices with their start and end apart: 17, of which 5 were waited for; matrix products, arithmetic and copies ran while one was open for 2% of the time, Pallas kernels for 0%

profile of v1, /device:TPU:0, one launch (start us, length us, event | category | flops | bytes accessed | tf_op | source)
XLA Modules:
  0.0 147.5 jit_solution(6353142195067069562)
XLA Ops:
  6.5 0.7 compare_select_fusion.7
  7.2 2.4 %scatter_custom_fusion.1 = s32[512]{0:T(512)S(1)} fusion(s32[512]{0:T(512)S(1)} %compare_select_fusion.7, s32[512]{0:T(512)S(1)} %iota.132, s32[]{:T(128)} %constant.506.clone.1), kind=kCustom, calls=%fused_computation.229 | custom fusion | bytes 2052 | tf_op jit(solution)/shard_map/scatter | solution.py:67
  10.2 0.6 broadcast.1156.clone
  10.8 2.2 %scatter_fusion.1 = f32[4,16,128]{2,0,1:T(4,128)} fusion(f32[4,16,128]{2,0,1:T(4,128)} %broadcast.1156.clone, s32[16]{0:T(128)S(1)} %get-tuple-element.484, f32[16,4,128]{2,1,0:T(4,128)S(1)} %bitcast.70), kind=kCustom, calls=%fused_computation.9 | custom fusion | bytes 98368 | tf_op jit(solution)/shard_map/scatter | solution.py:79
  13.0 8.4 %all-to-all-start = ((f32[4,16,128]{2,0,1:T(4,128)}), f32[4,16,128]{2,0,1:T(4,128)S(1)}, u32[]{:S(2)}, u32[]{:S(2)}) async-start(f32[4,16,128]{2,0,1:T(4,128)} %scatter_fusion.1), calls=%async_computation | async-start | bytes 65536 | tf_op jit(solution)/shard_map/all_to_all | solution.py:80
  21.6 0.7 gather_fusion.2
  22.8 0.8 gather_fusion.3
  23.9 4.9 %all-to-all-done = f32[4,16,128]{2,0,1:T(4,128)S(1)} async-done(((f32[4,16,128]{2,0,1:T(4,128)}), f32[4,16,128]{2,0,1:T(4,128)S(1)}, u32[]{:S(2)}, u32[]{:S(2)}) %all-to-all-start) | async-done | bytes 32800 | tf_op jit(solution)/shard_map/all_to_all | solution.py:80
  29.5 1.5 %scatter_fusion.2 = f32[4,16,128]{2,0,1:T(4,128)S(1)} fusion(f32[4,16,128]{2,0,1:T(4,128)S(1)} %broadcast.1156, s32[32]{0:T(128)S(1)} %get-tuple-element.485, f32[32,4,128]{2,1,0:T(4,128)S(1)} %gather_fusion.4), kind=kCustom, calls=%fused_computation.10 | custom fusion | bytes 196736 | tf_op jit(solution)/shard_map/scatter | solution.py:93
  31.0 1.9 %all_gather.15 = f32[4,32,128]{2,0,1:T(4,128)S(1)} all-gather(f32[4,16,128]{2,0,1:T(4,128)S(1)} %scatter_fusion.2), channel_id=1, replica_groups=mesh['brick'=16,'seed'=2] {'seed'}, dimensions={1}, use_global_device_ids=true | all-gather | bytes 98304 | tf_op jit(solution)/shard_map/all_gather | solution.py:94
  32.9 34.8 %while.35 = (s32[]{:T(128)}, f32[2,8,512]{2,1,0:T(8,128)S(1)}, f32[2,8,512]{2,1,0:T(8,128)S(1)}, s32[2]{0:T(128)S(1)}, pred[16,512]{1,0:T(8,128)(4,1)S(1)}, /*in...) while((s32[]{:T(128)}, f32[2,8,512]{2,1,0:T(8,128)S(1)}, ...), condition=%wide.region_8.9_spmd.clone, body=%wide.region_5.8_spmd.clone.sunk | while | flops 54553152 | bytes 820639 | solution.py:120
  34.2 0.6 gather_fusion
  35.4 4.3 %fusion.116 = f32[8,512]{1,0:T(8,128)S(1)} fusion(f32[8,512]{1,0:T(8,128)S(1)} %sub.611, f32[8,512]{1,0:T(8,128)S(1)} %broadcast_add_fusion.9, f32[8,512]{1,0:T(8,128)S(1)} %sub.612, f32[8,512]{1,0:T(8,128)S(1)} %broadcast_add_fusion.10, f32[8,512]{1,0:T(8,128)S(1)} %sub.613, f32[8,512]{1,0:T(8,128)S(1)} %broadcast_add_fusion.11, ...), kind=kLoop, calls=%fused_computation.16.clone.1 | loop fusion | flops 25161728 | bytes 135168 | tf_op jit(solution)/shard_map/while/body/eval_jaxpr/reduce_max | solution.py:115
  39.7 10.5 %select_reduce_fusion.2 = f32[8,512]{1,0:T(8,128)S(1)} fusion(f32[8,512]{1,0:T(8,128)S(1)} %fusion.116, f32[8,512]{1,0:T(8,128)S(1)} %sub.611, f32[8,512]{1,0:T(8,128)S(1)} %broadcast_add_fusion.9, f32[8,512]{1,0:T(8,128)S(1)} %sub.612, f32[8,512]{1,0:T(8,128)S(1)} %broadcast_add_fusion.10, f32[8,512]{1,0:T(8,128)S(1)} %sub.613, ...), kind=kLoop, calls=%fused_computation.14.clone.1 | loop fusion | flops 29356032 | bytes 151552 | tf_op jit(solution)/shard_map/while/body/eval_jaxpr/reduce_sum | solution.py:117
  51.6 0.6 gather_fusion
  52.8 4.3 %fusion.116 = f32[8,512]{1,0:T(8,128)S(1)} fusion(f32[8,512]{1,0:T(8,128)S(1)} %sub.611, f32[8,512]{1,0:T(8,128)S(1)} %broadcast_add_fusion.9, f32[8,512]{1,0:T(8,128)S(1)} %sub.612, f32[8,512]{1,0:T(8,128)S(1)} %broadcast_add_fusion.10, f32[8,512]{1,0:T(8,128)S(1)} %sub.613, f32[8,512]{1,0:T(8,128)S(1)} %broadcast_add_fusion.11, ...), kind=kLoop, calls=%fused_computation.16.clone.1 | loop fusion | flops 25161728 | bytes 135168 | tf_op jit(solution)/shard_map/while/body/eval_jaxpr/reduce_max | solution.py:115
  57.1 10.5 %select_reduce_fusion.2 = f32[8,512]{1,0:T(8,128)S(1)} fusion(f32[8,512]{1,0:T(8,128)S(1)} %fusion.116, f32[8,512]{1,0:T(8,128)S(1)} %sub.611, f32[8,512]{1,0:T(8,128)S(1)} %broadcast_add_fusion.9, f32[8,512]{1,0:T(8,128)S(1)} %sub.612, f32[8,512]{1,0:T(8,128)S(1)} %broadcast_add_fusion.10, f32[8,512]{1,0:T(8,128)S(1)} %sub.613, ...), kind=kLoop, calls=%fused_computation.14.clone.1 | loop fusion | flops 29356032 | bytes 151552 | tf_op jit(solution)/shard_map/while/body/eval_jaxpr/reduce_sum | solution.py:117
  67.6 1.9 %all-gather = f32[4,8,512]{2,1,0:T(8,128)S(1)} all-gather(f32[2,8,512]{2,1,0:T(8,128)S(1)} %get-tuple-element.338), channel_id=2, replica_groups=mesh['brick'=16,'seed'=2] {'seed'}, dimensions={0}, use_global_device_ids=true | all-gather | bytes 98304 | tf_op jit(solution)/shard_map/all_gather | solution.py:14
  69.5 1.8 %all-gather.1 = f32[4,8,512]{2,1,0:T(8,128)S(1)} all-gather(f32[2,8,512]{2,1,0:T(8,128)S(1)} %get-tuple-element.339), channel_id=3, replica_groups=mesh['brick'=16,'seed'=2] {'seed'}, dimensions={0}, use_global_device_ids=true | all-gather | bytes 98304 | tf_op jit(solution)/shard_map/all_gather | solution.py:14
  71.4 0.7 copy-done
  72.1 29.0 %while.36 = (s32[]{:T(128)}, f32[4,32,128]{2,0,1:T(4,128)S(1)}, s32[2]{0:T(128)S(1)}, s32[16,4]{1,0:T(8,128)S(1)}, pred[16,512]{1,0:T(8,128)(4,1)S(1)}, /*index=...) while((s32[]{:T(128)}, f32[4,32,128]{2,0,1:T(4,128)S(1)}, ...), condition=%wide.region_11.12_spmd.clone, body=%wide.region_9.11_spmd.clone.sunk | while | flops 130135552 | bytes 1242671 | solution.py:143
  74.7 10.3 %fusion.123 = f32[8,512,4]{1,2,0:T(4,128)S(1)} fusion(f32[8,512]{1,0:T(8,128)S(1)} %get-tuple-element.625, f32[8,512]{1,0:T(8,128)S(1)} %get-tuple-element.626, f32[8,512]{1,0:T(8,128)S(1)} %sub.631, f32[8,512]{1,0:T(8,128)S(1)} %get-tuple-element.633, f32[8,512]{1,0:T(8,128)S(1)} %sub.632, f32[8,512]{1,0:T(8,128)S(1)} %get-tuple-element.635, ...), kind=kOutput, calls=%fused_computation.78.clone.1 | convolution fusion | flops 130072576 | bytes 282624 | tf_op jit(solution)/shard_map/while/body/eval_jaxpr/fgi,gic->fgc/dot_general | solution.py:137
  84.9 1.7 %scatter_fusion = f32[4,32,128]{2,0,1:T(4,128)S(1)} fusion(f32[4,32,128]{2,0,1:T(4,128)S(1)} %get-tuple-element.697, s32[32]{0:T(128)S(1)} %fusion.118, f32[32,4,128]{2,1,0:T(4,128)S(1)} %bitcast.65), kind=kCustom, calls=%fused_computation.7.clone.clone.1 | custom fusion | flops 16384 | bytes 196736 | tf_op jit(solution)/shard_map/while/body/eval_jaxpr/scatter-add | solution.py:138
  88.3 0.6 gather_fusion.1
  89.1 10.3 %fusion.123 = f32[8,512,4]{1,2,0:T(4,128)S(1)} fusion(f32[8,512]{1,0:T(8,128)S(1)} %get-tuple-element.625, f32[8,512]{1,0:T(8,128)S(1)} %get-tuple-element.626, f32[8,512]{1,0:T(8,128)S(1)} %sub.631, f32[8,512]{1,0:T(8,128)S(1)} %get-tuple-element.633, f32[8,512]{1,0:T(8,128)S(1)} %sub.632, f32[8,512]{1,0:T(8,128)S(1)} %get-tuple-element.635, ...), kind=kOutput, calls=%fused_computation.78.clone.1 | convolution fusion | flops 130072576 | bytes 282624 | tf_op jit(solution)/shard_map/while/body/eval_jaxpr/fgi,gic->fgc/dot_general | solution.py:137
  99.4 1.7 %scatter_fusion = f32[4,32,128]{2,0,1:T(4,128)S(1)} fusion(f32[4,32,128]{2,0,1:T(4,128)S(1)} %get-tuple-element.697, s32[32]{0:T(128)S(1)} %fusion.118, f32[32,4,128]{2,1,0:T(4,128)S(1)} %bitcast.65), kind=kCustom, calls=%fused_computation.7.clone.clone.1 | custom fusion | flops 16384 | bytes 196736 | tf_op jit(solution)/shard_map/while/body/eval_jaxpr/scatter-add | solution.py:138
  101.1 0.6 gather_fusion.5
  101.7 1.5 %scatter_fusion.3 = f32[4,32,128]{2,0,1:T(4,128)S(1)} fusion(f32[4,32,128]{2,0,1:T(4,128)S(1)} %broadcast.1151, s32[32]{0:T(128)S(1)} %get-tuple-element.453, f32[32,4,128]{2,1,0:T(4,128)S(1)} %gather_fusion.5), kind=kCustom, calls=%fused_computation.11 | custom fusion | bytes 196736 | tf_op jit(solution)/shard_map/scatter | solution.py:146
  103.3 0.8 collective-permute-start
  104.2 1.4 collective-permute-start.1
  105.6 1.4 collective-permute-start.2
  107.0 1.4 collective-permute-start.3
  108.4 2.4 %collective-permute-start.4 = (f32[4,2,128]{2,0,1:T(4,128)S(1)}, f32[4,2,128]{2,0,1:T(4,128)S(1)}, u32[]{:S(2)}, u32[]{:S(2)}) collective-permute-start(f32[4,2,128]{2,0,1:T(4,128)S(1)} %get-tuple-element.478), channel_id=1, source_target_pairs={{0,22},{2,24},{4,26},{6,28},{8,30},{10,0},{12,2},{14,4},{16,6},{18... | collective-permute-start | bytes 12296 | tf_op jit(solution)/shard_map/ppermute | solution.py:158
  110.8 1.5 collective-permute-start.5
  112.3 1.4 collective-permute-start.6
  113.7 1.0 collective-permute-start.7
  114.7 3.7 %collective-permute-start.8 = (f32[4,2,128]{2,0,1:T(4,128)S(1)}, f32[4,2,128]{2,0,1:T(4,128)S(1)}, u32[]{:S(2)}, u32[]{:S(2)}) collective-permute-start(f32[4,2,128]{2,0,1:T(4,128)S(1)} %get-tuple-element.474), channel_id=1, source_target_pairs={{0,14},{2,16},{4,18},{6,20},{8,22},{10,24},{12,26},{14,28},{16,30}... | collective-permute-start | bytes 12296 | tf_op jit(solution)/shard_map/ppermute | solution.py:158
  118.4 1.5 %collective-permute-start.9 = (f32[4,2,128]{2,0,1:T(4,128)S(1)}, f32[4,2,128]{2,0,1:T(4,128)S(1)}, u32[]{:S(2)}, u32[]{:S(2)}) collective-permute-start(f32[4,2,128]{2,0,1:T(4,128)S(1)} %get-tuple-element.473), channel_id=1, source_target_pairs={{0,12},{2,14},{4,16},{6,18},{8,20},{10,22},{12,24},{14,26},{16,28}... | collective-permute-start | bytes 12296 | tf_op jit(solution)/shard_map/ppermute | solution.py:158
  120.0 1.6 %collective-permute-start.11 = (f32[4,2,128]{2,0,1:T(4,128)S(1)}, f32[4,2,128]{2,0,1:T(4,128)S(1)}, u32[]{:S(2)}, u32[]{:S(2)}) collective-permute-start(f32[4,2,128]{2,0,1:T(4,128)S(1)} %get-tuple-element.471), channel_id=1, source_target_pairs={{0,8},{2,10},{4,12},{6,14},{8,16},{10,18},{12,20},{14,22},{16,24},... | collective-permute-start | bytes 12296 | tf_op jit(solution)/shard_map/ppermute | solution.py:158
  121.6 3.6 %collective-permute-start.12 = (f32[4,2,128]{2,0,1:T(4,128)S(1)}, f32[4,2,128]{2,0,1:T(4,128)S(1)}, u32[]{:S(2)}, u32[]{:S(2)}) collective-permute-start(f32[4,2,128]{2,0,1:T(4,128)S(1)} %get-tuple-element.470), channel_id=1, source_target_pairs={{0,6},{2,8},{4,10},{6,12},{8,14},{10,16},{12,18},{14,20},{16,22},{... | collective-permute-start | bytes 12296 | tf_op jit(solution)/shard_map/ppermute | solution.py:158
  125.3 1.5 %collective-permute-start.13 = (f32[4,2,128]{2,0,1:T(4,128)S(1)}, f32[4,2,128]{2,0,1:T(4,128)S(1)}, u32[]{:S(2)}, u32[]{:S(2)}) collective-permute-start(f32[4,2,128]{2,0,1:T(4,128)S(1)} %get-tuple-element.469), channel_id=1, source_target_pairs={{0,4},{2,6},{4,8},{6,10},{8,12},{10,14},{12,16},{14,18},{16,20},{1... | collective-permute-start | bytes 12296 | tf_op jit(solution)/shard_map/ppermute | solution.py:158
  126.8 1.4 collective-permute-done.12
  128.2 3.4 %collective-permute-done.13 = f32[4,2,128]{2,0,1:T(4,128)S(1)} collective-permute-done((f32[4,2,128]{2,0,1:T(4,128)S(1)}, f32[4,2,128]{2,0,1:T(4,128)S(1)}, u32[]{:S(2)}, u32[]{:S(2)}) %collective-permute-start.13) | collective-permute-done | bytes 4128 | tf_op jit(solution)/shard_map/ppermute | solution.py:158
  131.6 2.4 %collective-permute-done.14 = f32[4,2,128]{2,0,1:T(4,128)S(1)} collective-permute-done((f32[4,2,128]{2,0,1:T(4,128)S(1)}, f32[4,2,128]{2,0,1:T(4,128)S(1)}, u32[]{:S(2)}, u32[]{:S(2)}) %collective-permute-start.14) | collective-permute-done | bytes 4128 | tf_op jit(solution)/shard_map/ppermute | solution.py:158
  134.1 0.6 copy.36
  134.7 3.9 %reduce-scatter.2.cloned.1.call-done = f32[4,16,1,128]{3,1,0,2:T(8,128)} async-done(((f32[4,16,2,128]{3,1,0,2:T(8,128)}), f32[4,16,1,128]{3,1,0,2:T(8,128)}) %reduce-scatter.2.cloned.1.call-update) | async-done | bytes 32784 | tf_op jit(solution)/shard_map/reduce_scatter | solution.py:168
  138.6 0.8 copy.37
  140.1 0.6 maximum_bitcast_fusion
  (169 shorter events, 8.4 us)
Async XLA Ops:
  9.8 1.0 copy-start.1
  13.0 8.5 %copy-start.2 = (s32[512]{0:T(512)S(1)}, s32[512]{0:T(512)}, u32[]{:S(2)}) copy-start(s32[512]{0:T(512)} %param.12) | copy-start | bytes 6148
  13.0 15.9 %all-to-all-start = ((f32[4,16,128]{2,0,1:T(4,128)}), f32[4,16,128]{2,0,1:T(4,128)S(1)}, u32[]{:S(2)}, u32[]{:S(2)}) async-start(f32[4,16,128]{2,0,1:T(4,128)} %scatter_fusion.1), calls=%async_computation | async-start | bytes 65536 | tf_op jit(solution)/shard_map/all_to_all | solution.py:80
  21.4 117.2 %reduce-scatter.2.cloned.1.call-start = ((), (), s32[]{:S(2)}) async-start(), calls=%async_computation.2 | async-start | bytes 98304 | tf_op jit(solution)/shard_map/reduce_scatter | solution.py:168
  21.6 1.0 copy-start.3
  22.8 0.9 copy-start.4
  71.4 0.8 copy-start
  103.3 7.5 %collective-permute-start = (f32[4,2,128]{2,0,1:T(4,128)S(1)}, f32[4,2,128]{2,0,1:T(4,128)S(1)}, u32[]{:S(2)}, u32[]{:S(2)}) collective-permute-start(f32[4,2,128]{2,0,1:T(4,128)S(1)} %get-tuple-element.482), channel_id=1, source_target_pairs={{0,30},{2,0},{4,2},{6,4},{8,6},{10,8},{12,10},{14,12},{16,14},{18,... | collective-permute-start | bytes 12296 | tf_op jit(solution)/shard_map/ppermute | solution.py:158
  104.2 8.1 %collective-permute-start.1 = (f32[4,2,128]{2,0,1:T(4,128)S(1)}, f32[4,2,128]{2,0,1:T(4,128)S(1)}, u32[]{:S(2)}, u32[]{:S(2)}) collective-permute-start(f32[4,2,128]{2,0,1:T(4,128)S(1)} %get-tuple-element.481), channel_id=1, source_target_pairs={{0,28},{2,30},{4,0},{6,2},{8,4},{10,6},{12,8},{14,10},{16,12},{18,... | collective-permute-start | bytes 12296 | tf_op jit(solution)/shard_map/ppermute | solution.py:158
  105.6 8.1 %collective-permute-start.2 = (f32[4,2,128]{2,0,1:T(4,128)S(1)}, f32[4,2,128]{2,0,1:T(4,128)S(1)}, u32[]{:S(2)}, u32[]{:S(2)}) collective-permute-start(f32[4,2,128]{2,0,1:T(4,128)S(1)} %get-tuple-element.480), channel_id=1, source_target_pairs={{0,26},{2,28},{4,30},{6,0},{8,2},{10,4},{12,6},{14,8},{16,10},{18,... | collective-permute-start | bytes 12296 | tf_op jit(solution)/shard_map/ppermute | solution.py:158
  107.0 7.7 %collective-permute-start.3 = (f32[4,2,128]{2,0,1:T(4,128)S(1)}, f32[4,2,128]{2,0,1:T(4,128)S(1)}, u32[]{:S(2)}, u32[]{:S(2)}) collective-permute-start(f32[4,2,128]{2,0,1:T(4,128)S(1)} %get-tuple-element.479), channel_id=1, source_target_pairs={{0,24},{2,26},{4,28},{6,30},{8,0},{10,2},{12,4},{14,6},{16,8},{18,... | collective-permute-start | bytes 12296 | tf_op jit(solution)/shard_map/ppermute | solution.py:158
  108.4 10.0 %collective-permute-start.4 = (f32[4,2,128]{2,0,1:T(4,128)S(1)}, f32[4,2,128]{2,0,1:T(4,128)S(1)}, u32[]{:S(2)}, u32[]{:S(2)}) collective-permute-start(f32[4,2,128]{2,0,1:T(4,128)S(1)} %get-tuple-element.478), channel_id=1, source_target_pairs={{0,22},{2,24},{4,26},{6,28},{8,30},{10,0},{12,2},{14,4},{16,6},{18... | collective-permute-start | bytes 12296 | tf_op jit(solution)/shard_map/ppermute | solution.py:158
  110.8 9.1 %collective-permute-start.5 = (f32[4,2,128]{2,0,1:T(4,128)S(1)}, f32[4,2,128]{2,0,1:T(4,128)S(1)}, u32[]{:S(2)}, u32[]{:S(2)}) collective-permute-start(f32[4,2,128]{2,0,1:T(4,128)S(1)} %get-tuple-element.477), channel_id=1, source_target_pairs={{0,20},{2,22},{4,24},{6,26},{8,28},{10,30},{12,0},{14,2},{16,4},{1... | collective-permute-start | bytes 12296 | tf_op jit(solution)/shard_map/ppermute | solution.py:158
  112.3 7.7 %collective-permute-start.6 = (f32[4,2,128]{2,0,1:T(4,128)S(1)}, f32[4,2,128]{2,0,1:T(4,128)S(1)}, u32[]{:S(2)}, u32[]{:S(2)}) collective-permute-start(f32[4,2,128]{2,0,1:T(4,128)S(1)} %get-tuple-element.476), channel_id=1, source_target_pairs={{0,18},{2,20},{4,22},{6,24},{8,26},{10,28},{12,30},{14,0},{16,2},{... | collective-permute-start | bytes 12296 | tf_op jit(solution)/shard_map/ppermute | solution.py:158
  113.7 7.9 %collective-permute-start.7 = (f32[4,2,128]{2,0,1:T(4,128)S(1)}, f32[4,2,128]{2,0,1:T(4,128)S(1)}, u32[]{:S(2)}, u32[]{:S(2)}) collective-permute-start(f32[4,2,128]{2,0,1:T(4,128)S(1)} %get-tuple-element.475), channel_id=1, source_target_pairs={{0,16},{2,18},{4,20},{6,22},{8,24},{10,26},{12,28},{14,30},{16,0},... | collective-permute-start | bytes 12296 | tf_op jit(solution)/shard_map/ppermute | solution.py:158
  114.7 10.6 %collective-permute-start.8 = (f32[4,2,128]{2,0,1:T(4,128)S(1)}, f32[4,2,128]{2,0,1:T(4,128)S(1)}, u32[]{:S(2)}, u32[]{:S(2)}) collective-permute-start(f32[4,2,128]{2,0,1:T(4,128)S(1)} %get-tuple-element.474), channel_id=1, source_target_pairs={{0,14},{2,16},{4,18},{6,20},{8,22},{10,24},{12,26},{14,28},{16,30}... | collective-permute-start | bytes 12296 | tf_op jit(solution)/shard_map/ppermute | solution.py:158
  118.4 8.3 %collective-permute-start.9 = (f32[4,2,128]{2,0,1:T(4,128)S(1)}, f32[4,2,128]{2,0,1:T(4,128)S(1)}, u32[]{:S(2)}, u32[]{:S(2)}) collective-permute-start(f32[4,2,128]{2,0,1:T(4,128)S(1)} %get-tuple-element.473), channel_id=1, source_target_pairs={{0,12},{2,14},{4,16},{6,18},{8,20},{10,22},{12,24},{14,26},{16,28}... | collective-permute-start | bytes 12296 | tf_op jit(solution)/shard_map/ppermute | solution.py:158
  120.0 6.8 %collective-permute-start.10 = (f32[4,2,128]{2,0,1:T(4,128)S(1)}, f32[4,2,128]{2,0,1:T(4,128)S(1)}, u32[]{:S(2)}, u32[]{:S(2)}) collective-permute-start(f32[4,2,128]{2,0,1:T(4,128)S(1)} %get-tuple-element.472), channel_id=1, source_target_pairs={{0,10},{2,12},{4,14},{6,16},{8,18},{10,20},{12,22},{14,24},{16,26}... | collective-permute-start | bytes 12296 | tf_op jit(solution)/shard_map/ppermute | solution.py:158
  120.0 6.8 %collective-permute-start.11 = (f32[4,2,128]{2,0,1:T(4,128)S(1)}, f32[4,2,128]{2,0,1:T(4,128)S(1)}, u32[]{:S(2)}, u32[]{:S(2)}) collective-permute-start(f32[4,2,128]{2,0,1:T(4,128)S(1)} %get-tuple-element.471), channel_id=1, source_target_pairs={{0,8},{2,10},{4,12},{6,14},{8,16},{10,18},{12,20},{14,22},{16,24},... | collective-permute-start | bytes 12296 | tf_op jit(solution)/shard_map/ppermute | solution.py:158
  121.6 6.6 %collective-permute-start.12 = (f32[4,2,128]{2,0,1:T(4,128)S(1)}, f32[4,2,128]{2,0,1:T(4,128)S(1)}, u32[]{:S(2)}, u32[]{:S(2)}) collective-permute-start(f32[4,2,128]{2,0,1:T(4,128)S(1)} %get-tuple-element.470), channel_id=1, source_target_pairs={{0,6},{2,8},{4,10},{6,12},{8,14},{10,16},{12,18},{14,20},{16,22},{... | collective-permute-start | bytes 12296 | tf_op jit(solution)/shard_map/ppermute | solution.py:158
  125.3 6.3 %collective-permute-start.13 = (f32[4,2,128]{2,0,1:T(4,128)S(1)}, f32[4,2,128]{2,0,1:T(4,128)S(1)}, u32[]{:S(2)}, u32[]{:S(2)}) collective-permute-start(f32[4,2,128]{2,0,1:T(4,128)S(1)} %get-tuple-element.469), channel_id=1, source_target_pairs={{0,4},{2,6},{4,8},{6,10},{8,12},{10,14},{12,16},{14,18},{16,20},{1... | collective-permute-start | bytes 12296 | tf_op jit(solution)/shard_map/ppermute | solution.py:158
  126.8 7.2 %collective-permute-start.14 = (f32[4,2,128]{2,0,1:T(4,128)S(1)}, f32[4,2,128]{2,0,1:T(4,128)S(1)}, u32[]{:S(2)}, u32[]{:S(2)}) collective-permute-start(f32[4,2,128]{2,0,1:T(4,128)S(1)} %get-tuple-element.468), channel_id=1, source_target_pairs={{0,2},{2,4},{4,6},{6,8},{8,10},{10,12},{12,14},{14,16},{16,18},{18... | collective-permute-start | bytes 12296 | tf_op jit(solution)/shard_map/ppermute | solution.py:158
Sparse Core Ops, SparseCore 0:
  134.9 3.7 reduce-scatter.1
